TPU v7x, 32 devices: a whole 2x2x4 slice. The times are simulated.
32 devices in a mesh: dp: 4 (over x, core), group: 8 (over z, y).
Axes of the slice: x: 2, y: 2, z: 4, core: 2. Of those that a mesh axis runs over, the one named last changes fastest.
Arguments:
- image_tiles: bfloat16 [4, 8, 8, 4, 4, 352], P('dp', 'group'), may hold values from -6 to 6
- cotangent: bfloat16 [4, 8, 8, 4, 4, 352], P('dp', 'group'), may hold values from -6 to 6
- image_rows: int32 [4, 8], P('dp', 'group'), may hold values from 1 to 2, as said below
- dw_kernel: float32 [7, 7, 352], replicated, may hold values from -0.875 to 0.875
- dw_bias: float32 [352], replicated, may hold values from -1 to 1
- layer_norm_gain: float32 [352], replicated, may hold values from 0.1 to 1.9
- layer_norm_bias: float32 [352], replicated, may hold values from -3 to 3
- weight_in: bfloat16 [352, 1408], replicated, may hold values from -0.3125 to 0.3125
- bias_in: float32 [1408], replicated, may hold values from -2.5 to 1
- grn_gamma: float32 [1408], replicated, may hold values from -1 to 1
- grn_beta: float32 [1408], replicated, may hold values from -3 to 3
- weight_out: bfloat16 [1408, 352], replicated, may hold values from -0.15625 to 0.15625
- bias_out: float32 [352], replicated, may hold values from -3 to 3
Outputs:
- outputs: bfloat16 [4, 8, 8, 4, 4, 352], P('dp', 'group')
- input_grads: bfloat16 [4, 8, 8, 4, 4, 352], P('dp', 'group')
- grad_shards: float32 [32, 31696], P(('dp', 'group'))
Inputs may be any that keep to these rules, and one draw needn't show every extreme that they name: `image_rows`: some device's image has all 2 tile rows.
All inputs are finite; a program needn't handle non-finite values.
Results may differ from a plain program's by a relative error of at most 0.0051.
Values may be sent and summed in bfloat16 or wider, within the bound.
No kernel may reach another device: no remote copies, remote signals or barrier semaphores. Data moves between devices by JAX's collectives and lax.ppermute only.
A program may use at most 64 MiB of HBM per device.

v0:
```python
import math
import jax
import jax.numpy as jnp
from jax import lax
from jax.sharding import PartitionSpec as P

GC = 4


def image_step(
    inputs,
    upstream,
    valid,
    dw_kernel,
    dw_bias,
    layer_norm_gain,
    layer_norm_bias,
    weight_in,
    bias_in,
    grn_gamma,
    grn_beta,
    weight_out,
    bias_out,
):
    height, width, channel_count = inputs.shape
    hidden_dim = weight_in.shape[1]
    total_row_count = height * width
    cell_mask = jnp.broadcast_to(valid, (height, width, 1)).reshape(total_row_count, 1)
    float_in = inputs.astype(jnp.float32)
    padded_in = jnp.pad(float_in, ((3, 3), (3, 3), (0, 0)))
    conv_out = jnp.zeros_like(float_in) + dw_bias
    for row_off in range(7):
        for col_off in range(7):
            conv_out = (
                conv_out
                + padded_in[row_off : row_off + height, col_off : col_off + width, :]
                * dw_kernel[row_off, col_off]
            )
    mean_c = jnp.mean(conv_out, axis=-1, keepdims=True)
    centered_values = conv_out - mean_c
    inverse_deviation = lax.rsqrt(
        jnp.mean(centered_values * centered_values, axis=-1, keepdims=True) + 1e-06
    )
    standardized_input = centered_values * inverse_deviation
    normalized_output = (
        (standardized_input * layer_norm_gain + layer_norm_bias)
        .astype(jnp.bfloat16)
        .reshape(total_row_count, channel_count)
    )
    pre_act = jnp.dot(normalized_output, weight_in, preferred_element_type=jnp.float32) + bias_in
    act_out = 0.5 * pre_act * (1.0 + lax.erf(pre_act * 0.7071067811865476))
    act_kept = act_out * cell_mask
    norm_val = jnp.sqrt(1.0 + jnp.sum(act_kept * act_kept, axis=0, keepdims=True))
    denom = jnp.mean(norm_val, axis=-1, keepdims=True) + 1e-06
    scale_val = norm_val / denom
    mixed = (grn_gamma * (act_out * scale_val) + grn_beta + act_out).astype(jnp.bfloat16)
    branch = jnp.dot(mixed, weight_out, preferred_element_type=jnp.float32) + bias_out
    whole = float_in.reshape(total_row_count, channel_count) + branch
    result = (
        jnp.where(cell_mask > 0, whole, jnp.zeros_like(whole))
        .astype(jnp.bfloat16)
        .reshape(inputs.shape)
    )
    up_rows = upstream.reshape(total_row_count, channel_count)
    up_float = up_rows.astype(jnp.float32)
    g_bias_out = jnp.sum(up_float, axis=0)
    g_weight_out = lax.dot_general(
        mixed, up_rows, (((0,), (0,)), ((), ())), preferred_element_type=jnp.float32
    )
    d_mixed = lax.dot_general(
        up_rows, weight_out, (((1,), (1,)), ((), ())), preferred_element_type=jnp.float32
    )
    g_gamma = jnp.sum(d_mixed * act_out * scale_val, axis=0)
    g_beta = jnp.sum(d_mixed, axis=0)
    d_scale = jnp.sum(d_mixed * grn_gamma * act_out, axis=0, keepdims=True)
    d_norm = (
        d_scale / denom
        - jnp.sum(d_scale * norm_val, axis=-1, keepdims=True) / (denom * denom) / hidden_dim
    )
    d_act = d_mixed * (grn_gamma * scale_val + 1.0) + act_kept * d_norm / norm_val
    cdf_val = 0.5 * (1.0 + lax.erf(pre_act * 0.7071067811865476))
    pdf_val = jnp.exp(-0.5 * pre_act * pre_act) * 0.3989422804014327
    d_pre = d_act * (cdf_val + pre_act * pdf_val)
    g_bias_in = jnp.sum(d_pre, axis=0)
    d_pre_b = d_pre.astype(jnp.bfloat16)
    g_weight_in = lax.dot_general(
        normalized_output, d_pre_b, (((0,), (0,)), ((), ())), preferred_element_type=jnp.float32
    )
    normalized_gradient = lax.dot_general(
        d_pre_b, weight_in, (((1,), (1,)), ((), ())), preferred_element_type=jnp.float32
    ).reshape(inputs.shape)
    layer_norm_gain_gradient = jnp.sum(normalized_gradient * standardized_input, axis=(0, 1))
    g_ln_bias = jnp.sum(normalized_gradient, axis=(0, 1))
    upscaled_values = normalized_gradient * layer_norm_gain
    conv_output_gradient = inverse_deviation * (
        upscaled_values
        - jnp.mean(upscaled_values, axis=-1, keepdims=True)
        - standardized_input
        * jnp.mean(upscaled_values * standardized_input, axis=-1, keepdims=True)
    )
    g_dw_bias = jnp.sum(conv_output_gradient, axis=(0, 1))
    padded_grad = jnp.pad(conv_output_gradient, ((3, 3), (3, 3), (0, 0)))
    back_float = up_float.reshape(inputs.shape)
    kernel_rows = []
    for row_off in range(7):
        for col_off in range(7):
            kernel_rows.append(
                jnp.sum(
                    padded_in[row_off : row_off + height, col_off : col_off + width, :]
                    * conv_output_gradient,
                    axis=(0, 1),
                )
            )
            back_float = (
                back_float
                + padded_grad[
                    6 - row_off : 6 - row_off + height, 6 - col_off : 6 - col_off + width, :
                ]
                * dw_kernel[row_off, col_off]
            )
    back_float = jnp.where(valid > 0, back_float, jnp.zeros_like(back_float))
    g_kernel = jnp.stack(kernel_rows)
    grad_flat = jnp.concatenate(
        [
            g_kernel.reshape(-1),
            g_dw_bias,
            layer_norm_gain_gradient,
            g_ln_bias,
            g_weight_in.reshape(-1),
            g_bias_in,
            g_gamma,
            g_beta,
            g_weight_out.reshape(-1),
            g_bias_out,
        ]
    )
    return (result, back_float.astype(jnp.bfloat16), grad_flat)


def to_canvas(tiles, grid_rows, grid_cols):
    slot_count, tile_h, tile_w, channel_count = tiles.shape
    return (
        tiles.reshape(grid_rows, grid_cols, tile_h, tile_w, channel_count)
        .transpose(0, 2, 1, 3, 4)
        .reshape(grid_rows * tile_h, grid_cols * tile_w, channel_count)
    )


def to_tiles(canvas, grid_rows, grid_cols, tile_h, tile_w):
    channel_count = canvas.shape[-1]
    return (
        canvas.reshape(grid_rows, tile_h, grid_cols, tile_w, channel_count)
        .transpose(0, 2, 1, 3, 4)
        .reshape(grid_rows * grid_cols, tile_h, tile_w, channel_count)
    )


def per_device(
    image_tiles,
    cotangent,
    image_rows,
    dw_kernel,
    dw_bias,
    layer_norm_gain,
    layer_norm_bias,
    weight_in,
    bias_in,
    grn_gamma,
    grn_beta,
    weight_out,
    bias_out,
):
    received = lax.all_to_all(image_tiles, "group", split_axis=2, concat_axis=2, tiled=True)
    tiles = received[0, 0]
    slot_count, tile_h, tile_w, channel_count = tiles.shape
    grid_rows = slot_count // GC
    cell_rows = jnp.arange(grid_rows * tile_h, dtype=jnp.int32) // tile_h
    valid = (cell_rows < image_rows[0, 0]).astype(jnp.float32).reshape(grid_rows * tile_h, 1, 1)
    canvas = to_canvas(tiles, grid_rows, GC)
    canvas = jnp.where(valid > 0, canvas, jnp.zeros_like(canvas))
    up_canvas = to_canvas(cotangent[0, 0], grid_rows, GC)
    up_canvas = jnp.where(valid > 0, up_canvas, jnp.zeros_like(up_canvas))
    params = (
        dw_kernel,
        dw_bias,
        layer_norm_gain,
        layer_norm_bias,
        weight_in,
        bias_in,
        grn_gamma,
        grn_beta,
        weight_out,
        bias_out,
    )
    result, back_grads, grad_flat = image_step(canvas, up_canvas, valid, *params)
    outputs = to_tiles(result, grid_rows, GC, tile_h, tile_w)
    back_tiles = to_tiles(back_grads, grid_rows, GC, tile_h, tile_w)
    returned = lax.all_to_all(
        back_tiles[None, None], "group", split_axis=2, concat_axis=2, tiled=True
    )
    data_count = lax.axis_size("dp")
    group_count = lax.axis_size("group")
    devices_all = data_count * group_count
    total_len = grad_flat.shape[0]
    shard_len = (total_len + 8 * devices_all - 1) // (8 * devices_all) * 8
    padded = jnp.pad(grad_flat, (0, devices_all * shard_len - total_len))
    factor = 1.0 / math.sqrt(data_count * group_count * group_count * tile_h * tile_w)
    owned = lax.psum_scatter(
        padded.reshape(devices_all, shard_len), ("dp", "group"), scatter_dimension=0, tiled=True
    )
    return (outputs[None, None], returned, owned * factor)


def solution(mesh):
    return jax.shard_map(
        per_device,
        mesh=mesh,
        in_specs=(
            P("dp", "group", None, None, None, None),
            P("dp", "group", None, None, None, None),
            P("dp", "group"),
            P(),
            P(),
            P(),
            P(),
            P(),
            P(),
            P(),
            P(),
            P(),
            P(),
        ),
        out_specs=(
            P("dp", "group", None, None, None, None),
            P("dp", "group", None, None, None, None),
            P(("dp", "group"), None),
        ),
        check_vma=False,
    )
```

profile of v0, /device:TPU:0, one launch (start us, length us, event | category | flops | bytes accessed | tf_op | source)
XLA Modules:
  0.0 254.1 jit_solution(9716714760860221564)
XLA Ops:
  7.2 0.0 copy-start
  7.2 0.0 copy-start.84
  7.2 7.5 %all-to-all-start = ((bf16[1,1,8,4,4,352]{5,4,3,1,0,2:T(4,128)(2,1)}), bf16[1,1,8,4,4,352]{5,4,3,1,0,2:T(4,128)(2,1)S(1)}, u32[]{:S(2)}, u32[]{:S(2)}) async-start(bf16[1,1,8,4,4,352]{5,4,3,1,0,2:T(4,128)(2,1)} %bitcast.47), calls=%async_computation | async-start | bytes 196608 | tf_op jit(solution)/shard_map/all_to_all | solution.py:173
  14.7 0.0 all-reduce.6.cloned.1.call-start
  14.7 1.0 slice_reduce_fusion.46
  15.8 1.3 slice_reduce_fusion.48
  17.2 1.9 slice_reduce_fusion.47
  19.8 0.5 compare_convert_fusion.1
  20.3 0.6 broadcast_in_dim.67
  20.9 0.6 broadcast_in_dim.68
  21.6 0.1 broadcast_in_dim.64
  21.6 0.6 broadcast_in_dim.65
  22.3 0.9 copy.53
  23.2 0.1 reshape.172
  23.3 0.1 copy.42
  23.4 0.0 copy-start.3
  23.4 1.6 convert_reduce_fusion
  25.1 0.0 all-to-all-done
  25.1 0.1 reshape.169
  25.1 0.0 copy-start.1
  25.2 0.7 select_convert_fusion
  25.8 2.2 fusion.123
  28.0 0.2 multiply_reduce_fusion.54
  28.2 0.1 add_convert_fusion.1
  28.6 1.1 multiply_reduce_fusion.2
  29.8 0.7 fusion.118
  31.1 2.5 %multiply_reduce_fusion = (f32[1408]{0:T(1024)S(1)}, f32[1408]{0:T(1024)S(1)}, f32[1408]{0:T(1024)S(1)}, f32[128,1408]{1,0:T(8,128)}) fusion(f32[128,1408]{1,0:T(8,128)S(1)} %get-tuple-element.130, f32[1408]{0:T(1024)S(1)} %get-tuple-element.128, f32[1408]{0:T(1024)S(1)} %copy-done.5, bf16[1408,352]{0,1:T(8,128)(2,1)} %param.24, ...), kind=kOutput, calls=%fused_computation.107 | convolution fusion | flops 128180096 | bytes 2551424 | tf_op jit(solution)/shard_map/dot_general | solution.py:70
  33.7 0.7 multiply_reduce_fusion.56
  35.0 1.6 fusion.121
  36.6 0.0 copy-start.2
  36.6 0.5 fusion.120
  37.2 0.1 copy.43
  37.3 0.2 multiply_reduce_fusion.3
  37.5 0.1 div.84
  37.6 0.6 multiply_reduce_fusion.4
  38.2 0.9 fusion.119
  39.1 0.4 multiply_reduce_fusion.22
  39.5 1.7 fusion.107
  41.6 0.0 copy-start.4
  41.7 0.0 copy-start.82
  41.8 0.2 stack.199
  42.0 0.1 reshape.175
  42.1 2.8 %reshape.176 = f32[495616]{0:T(1024)} reshape(f32[352,1408]{1,0:T(8,128)} %fusion.107) | data formatting | bytes 3964928 | tf_op jit(solution)/shard_map/reshape | solution.py:129
  44.9 2.5 fusion.111
  47.4 4.0 %reshape.177 = f32[495616]{0:T(1024)} reshape(f32[1408,352]{1,0:T(8,128)} %fusion.111) | data formatting | bytes 3964928 | tf_op jit(solution)/shard_map/reshape | solution.py:133
  51.3 37.9 %concatenate.3 = f32[1014112]{0:T(1024)} concatenate(f32[17248]{0:T(1024)S(1)} %reshape.175, f32[352]{0:T(512)S(1)} %get-tuple-element.59, f32[352]{0:T(512)S(1)} %get-tuple-element.57, f32[352]{0:T(512)S(1)} %get-tuple-element.73, f32[495616]{0:T(1024)} %reshape.176, f32[1408]{0:T(1024)S(1)} %get-tuple-element.124, f32[1408]{0:T(1024)S(1)} %get-tuple-element.6, ...), dimensions={0} | concatenate | bytes 8112896 | tf_op jit(solution)/shard_map/concatenate | solution.py:123
  89.2 4.3 %pad.13 = f32[1014272]{0:T(1024)} pad(f32[1014112]{0:T(1024)} %concatenate.3, f32[]{:T(128)} %constant.50.clone.1), padding=0_160 | pad | bytes 8113540 | tf_op jit(solution)/shard_map/jit(_pad)/pad | solution.py:206
  93.5 6.4 %reshape.178 = f32[32,31696]{1,0:T(8,128)} reshape(f32[1014272]{0:T(1024)} %pad.13) | data formatting | bytes 8114176 | tf_op jit(solution)/shard_map/reshape | solution.py:209
  100.2 0.0 copy-start.85
  100.3 0.0 all-reduce.6.cloned.1.call-update
  100.3 0.1 reshape.171
  100.3 0.7 broadcast_compare_fusion.1
  101.0 0.1 reshape.168
  101.1 0.1 copy.38
  101.6 2.1 fusion.100
  103.7 0.7 copy.44
  104.4 6.0 %all-to-all-start.1 = ((bf16[1,1,8,4,4,352]{5,4,3,1,0,2:T(4,128)(2,1)}), bf16[1,1,8,4,4,352]{5,4,3,1,0,2:T(4,128)(2,1)S(1)}, u32[]{:S(2)}, u32[]{:S(2)}) async-start(bf16[1,1,8,4,4,352]{5,4,3,1,0,2:T(4,128)(2,1)} %bitcast.12), calls=%async_computation.1 | async-start | bytes 196608 | tf_op jit(solution)/shard_map/all_to_all | solution.py:198
  110.3 1.7 fusion.2
  112.0 0.1 copy.39
  112.2 0.7 copy.40
  112.9 5.8 %all-to-all-done.1 = bf16[1,1,8,4,4,352]{5,4,3,1,0,2:T(4,128)(2,1)S(1)} async-done(((bf16[1,1,8,4,4,352]{5,4,3,1,0,2:T(4,128)(2,1)}), bf16[1,1,8,4,4,352]{5,4,3,1,0,2:T(4,128)(2,1)S(1)}, u32[]{:S(2)}, u32[]{:S(2)}) %all-to-all-start.1) | async-done | bytes 90144 | tf_op jit(solution)/shard_map/all_to_all | solution.py:198
  118.7 125.9 %all-reduce.6.cloned.1.call-done = f32[32,31696]{1,0:T(8,128)} async-done(((f32[32,31696]{1,0:T(8,128)}), f32[32,31696]{1,0:T(8,128)}) %all-reduce.6.cloned.1.call-update) | async-done | bytes 4057104
  244.6 2.0 dynamic-slice_multiply_fusion
  246.6 0.6 copy.58
  (223 shorter events, 0.7 us)
Async XLA Ops:
  7.2 21.4 %copy-start = (bf16[352,1408]{1,0:T(8,128)(2,1)S(1)}, bf16[352,1408]{1,0:T(8,128)(2,1)}, u32[]{:S(2)}) copy-start(bf16[352,1408]{1,0:T(8,128)(2,1)} %param.20) | copy-start | bytes 2973700
  7.2 21.0 %copy-start.84 = (f32[352]{0:T(512)S(1)}, f32[352]{0:T(512)}, u32[]{:S(2)}) copy-start(f32[352]{0:T(512)} %param.19) | copy-start | bytes 4228
  7.2 21.0 %copy-start.6 = (f32[352]{0:T(512)S(1)}, f32[352]{0:T(512)}, u32[]{:S(2)}) copy-start(f32[352]{0:T(512)} %param.18) | copy-start | bytes 4228
  7.2 21.4 %copy-start.81 = (f32[1408]{0:T(1024)S(1)}, f32[1408]{0:T(1024)}, u32[]{:S(2)}) copy-start(f32[1408]{0:T(1024)} %param.21) | copy-start | bytes 16900
  7.2 17.8 %all-to-all-start = ((bf16[1,1,8,4,4,352]{5,4,3,1,0,2:T(4,128)(2,1)}), bf16[1,1,8,4,4,352]{5,4,3,1,0,2:T(4,128)(2,1)S(1)}, u32[]{:S(2)}, u32[]{:S(2)}) async-start(bf16[1,1,8,4,4,352]{5,4,3,1,0,2:T(4,128)(2,1)} %bitcast.47), calls=%async_computation | async-start | bytes 196608 | tf_op jit(solution)/shard_map/all_to_all | solution.py:173
  14.7 229.9 %all-reduce.6.cloned.1.call-start = ((), (), s32[]{:S(2)}) async-start(), calls=%async_computation.2 | async-start | bytes 8126464
  15.7 12.3 %copy-start.7 = (f32[352]{0:T(512)}, f32[352]{0:T(512)S(1)}, u32[]{:S(2)}) copy-start(f32[352]{0:T(512)S(1)} %get-tuple-element.114) | copy-start | bytes 4228
  15.7 12.3 %copy-start.13 = (f32[352]{0:T(512)}, f32[352]{0:T(512)S(1)}, u32[]{:S(2)}) copy-start(f32[352]{0:T(512)S(1)} %get-tuple-element.117) | copy-start | bytes 4228
  15.7 14.0 %copy-start.9 = (f32[352]{0:T(512)}, f32[352]{0:T(512)S(1)}, u32[]{:S(2)}) copy-start(f32[352]{0:T(512)S(1)} %get-tuple-element.115) | copy-start | bytes 4228
  15.7 14.0 %copy-start.11 = (f32[352]{0:T(512)}, f32[352]{0:T(512)S(1)}, u32[]{:S(2)}) copy-start(f32[352]{0:T(512)S(1)} %get-tuple-element.116) | copy-start | bytes 4228
  15.7 14.0 %copy-start.15 = (f32[352]{0:T(512)}, f32[352]{0:T(512)S(1)}, u32[]{:S(2)}) copy-start(f32[352]{0:T(512)S(1)} %get-tuple-element.118) | copy-start | bytes 4228
  15.7 14.0 %copy-start.17 = (f32[352]{0:T(512)}, f32[352]{0:T(512)S(1)}, u32[]{:S(2)}) copy-start(f32[352]{0:T(512)S(1)} %get-tuple-element.119) | copy-start | bytes 4228
  15.7 14.0 %copy-start.19 = (f32[352]{0:T(512)}, f32[352]{0:T(512)S(1)}, u32[]{:S(2)}) copy-start(f32[352]{0:T(512)S(1)} %get-tuple-element.120) | copy-start | bytes 4228
  15.7 14.0 %copy-start.21 = (f32[352]{0:T(512)}, f32[352]{0:T(512)S(1)}, u32[]{:S(2)}) copy-start(f32[352]{0:T(512)S(1)} %get-tuple-element.121) | copy-start | bytes 4228
  15.8 14.0 %copy-start.23 = (f32[352]{0:T(512)}, f32[352]{0:T(512)S(1)}, u32[]{:S(2)}) copy-start(f32[352]{0:T(512)S(1)} %get-tuple-element.122) | copy-start | bytes 4228
  15.8 14.0 %copy-start.25 = (f32[352]{0:T(512)}, f32[352]{0:T(512)S(1)}, u32[]{:S(2)}) copy-start(f32[352]{0:T(512)S(1)} %get-tuple-element.123) | copy-start | bytes 4228
  17.1 11.3 %copy-start.35 = (f32[352]{0:T(512)}, f32[352]{0:T(512)S(1)}, u32[]{:S(2)}) copy-start(f32[352]{0:T(512)S(1)} %get-tuple-element.79) | copy-start | bytes 4228
  17.1 11.3 %copy-start.37 = (f32[352]{0:T(512)}, f32[352]{0:T(512)S(1)}, u32[]{:S(2)}) copy-start(f32[352]{0:T(512)S(1)} %get-tuple-element.80) | copy-start | bytes 4228
  17.1 11.3 %copy-start.39 = (f32[352]{0:T(512)}, f32[352]{0:T(512)S(1)}, u32[]{:S(2)}) copy-start(f32[352]{0:T(512)S(1)} %get-tuple-element.81) | copy-start | bytes 4228
  17.1 11.3 %copy-start.41 = (f32[352]{0:T(512)}, f32[352]{0:T(512)S(1)}, u32[]{:S(2)}) copy-start(f32[352]{0:T(512)S(1)} %get-tuple-element.82) | copy-start | bytes 4228
  17.1 11.3 %copy-start.43 = (f32[352]{0:T(512)}, f32[352]{0:T(512)S(1)}, u32[]{:S(2)}) copy-start(f32[352]{0:T(512)S(1)} %get-tuple-element.83) | copy-start | bytes 4228
  17.1 11.3 %copy-start.45 = (f32[352]{0:T(512)}, f32[352]{0:T(512)S(1)}, u32[]{:S(2)}) copy-start(f32[352]{0:T(512)S(1)} %get-tuple-element.84) | copy-start | bytes 4228
  17.1 11.3 %copy-start.47 = (f32[352]{0:T(512)}, f32[352]{0:T(512)S(1)}, u32[]{:S(2)}) copy-start(f32[352]{0:T(512)S(1)} %get-tuple-element.85) | copy-start | bytes 4228
  17.1 11.3 %copy-start.49 = (f32[352]{0:T(512)}, f32[352]{0:T(512)S(1)}, u32[]{:S(2)}) copy-start(f32[352]{0:T(512)S(1)} %get-tuple-element.86) | copy-start | bytes 4228
  17.1 11.3 %copy-start.51 = (f32[352]{0:T(512)}, f32[352]{0:T(512)S(1)}, u32[]{:S(2)}) copy-start(f32[352]{0:T(512)S(1)} %get-tuple-element.87) | copy-start | bytes 4228
  17.1 11.3 %copy-start.53 = (f32[352]{0:T(512)}, f32[352]{0:T(512)S(1)}, u32[]{:S(2)}) copy-start(f32[352]{0:T(512)S(1)} %get-tuple-element.88) | copy-start | bytes 4228
  17.2 11.3 %copy-start.55 = (f32[352]{0:T(512)}, f32[352]{0:T(512)S(1)}, u32[]{:S(2)}) copy-start(f32[352]{0:T(512)S(1)} %get-tuple-element.89) | copy-start | bytes 4228
  17.2 11.3 %copy-start.57 = (f32[352]{0:T(512)}, f32[352]{0:T(512)S(1)}, u32[]{:S(2)}) copy-start(f32[352]{0:T(512)S(1)} %get-tuple-element.90) | copy-start | bytes 4228
  17.2 11.3 %copy-start.59 = (f32[352]{0:T(512)}, f32[352]{0:T(512)S(1)}, u32[]{:S(2)}) copy-start(f32[352]{0:T(512)S(1)} %get-tuple-element.91) | copy-start | bytes 4228
  17.2 11.3 %copy-start.61 = (f32[352]{0:T(512)}, f32[352]{0:T(512)S(1)}, u32[]{:S(2)}) copy-start(f32[352]{0:T(512)S(1)} %get-tuple-element.92) | copy-start | bytes 4228
  17.2 11.3 %copy-start.63 = (f32[352]{0:T(512)}, f32[352]{0:T(512)S(1)}, u32[]{:S(2)}) copy-start(f32[352]{0:T(512)S(1)} %get-tuple-element.93) | copy-start | bytes 4228
  17.2 12.6 %copy-start.27 = (f32[352]{0:T(512)}, f32[352]{0:T(512)S(1)}, u32[]{:S(2)}) copy-start(f32[352]{0:T(512)S(1)} %get-tuple-element.75) | copy-start | bytes 4228
  17.2 12.6 %copy-start.29 = (f32[352]{0:T(512)}, f32[352]{0:T(512)S(1)}, u32[]{:S(2)}) copy-start(f32[352]{0:T(512)S(1)} %get-tuple-element.76) | copy-start | bytes 4228
  17.2 12.6 %copy-start.31 = (f32[352]{0:T(512)}, f32[352]{0:T(512)S(1)}, u32[]{:S(2)}) copy-start(f32[352]{0:T(512)S(1)} %get-tuple-element.77) | copy-start | bytes 4228
  17.2 12.6 %copy-start.33 = (f32[352]{0:T(512)}, f32[352]{0:T(512)S(1)}, u32[]{:S(2)}) copy-start(f32[352]{0:T(512)S(1)} %get-tuple-element.78) | copy-start | bytes 4228
  19.1 9.4 %copy-start.65 = (f32[352]{0:T(512)}, f32[352]{0:T(512)S(1)}, u32[]{:S(2)}) copy-start(f32[352]{0:T(512)S(1)} %get-tuple-element.94) | copy-start | bytes 4228
  19.1 9.4 %copy-start.67 = (f32[352]{0:T(512)}, f32[352]{0:T(512)S(1)}, u32[]{:S(2)}) copy-start(f32[352]{0:T(512)S(1)} %get-tuple-element.95) | copy-start | bytes 4228
  19.1 9.4 %copy-start.69 = (f32[352]{0:T(512)}, f32[352]{0:T(512)S(1)}, u32[]{:S(2)}) copy-start(f32[352]{0:T(512)S(1)} %get-tuple-element.96) | copy-start | bytes 4228
  19.1 9.4 %copy-start.71 = (f32[352]{0:T(512)}, f32[352]{0:T(512)S(1)}, u32[]{:S(2)}) copy-start(f32[352]{0:T(512)S(1)} %get-tuple-element.97) | copy-start | bytes 4228
  19.1 9.4 %copy-start.73 = (f32[352]{0:T(512)}, f32[352]{0:T(512)S(1)}, u32[]{:S(2)}) copy-start(f32[352]{0:T(512)S(1)} %get-tuple-element.98) | copy-start | bytes 4228
  19.1 9.4 %copy-start.75 = (f32[352]{0:T(512)}, f32[352]{0:T(512)S(1)}, u32[]{:S(2)}) copy-start(f32[352]{0:T(512)S(1)} %get-tuple-element.99) | copy-start | bytes 4228
  19.1 9.4 %copy-start.77 = (f32[352]{0:T(512)}, f32[352]{0:T(512)S(1)}, u32[]{:S(2)}) copy-start(f32[352]{0:T(512)S(1)} %get-tuple-element.100) | copy-start | bytes 4228
  19.1 9.4 %copy-start.79 = (f32[352]{0:T(512)}, f32[352]{0:T(512)S(1)}, u32[]{:S(2)}) copy-start(f32[352]{0:T(512)S(1)} %get-tuple-element.101) | copy-start | bytes 4228
  23.4 7.7 %copy-start.3 = (bf16[128,352]{0,1:T(8,128)(2,1)}, bf16[128,352]{0,1:T(8,128)(2,1)S(1)}, u32[]{:S(2)}) copy-start(bf16[128,352]{0,1:T(8,128)(2,1)S(1)} %copy.42) | copy-start | bytes 270340
  25.1 6.1 %copy-start.5 = (f32[1408]{0:T(1024)S(1)}, f32[1408]{0:T(1024)}, u32[]{:S(2)}) copy-start(f32[1408]{0:T(1024)} %param.22) | copy-start | bytes 16900
  25.1 3.4 %copy-start.1 = (bf16[8,16,352]{2,1,0:T(8,128)(2,1)}, bf16[8,16,352]{2,1,0:T(8,128)(2,1)S(1)}, u32[]{:S(2)}) copy-start(bf16[8,16,352]{2,1,0:T(8,128)(2,1)S(1)} %reshape.169) | copy-start | bytes 270340
  36.6 1.6 copy-start.2
  41.6 3.2 %copy-start.4 = (bf16[128,352]{0,1:T(8,128)(2,1)S(1)}, bf16[128,352]{0,1:T(8,128)(2,1)}, u32[]{:S(2)}) copy-start(bf16[128,352]{0,1:T(8,128)(2,1)} %copy-done.3) | copy-start | bytes 270340
  41.7 3.2 %copy-start.82 = (f32[1408]{0:T(1024)S(1)}, f32[1408]{0:T(1024)}, u32[]{:S(2)}) copy-start(f32[1408]{0:T(1024)} %param.23) | copy-start | bytes 16900
  47.4 4.0 %copy-start.83 = (f32[352]{0:T(512)S(1)}, f32[352]{0:T(512)}, u32[]{:S(2)}) copy-start(f32[352]{0:T(512)} %convert_reduce_fusion) | copy-start | bytes 4228
  99.9 1.3 copy-start.16
  99.9 1.3 copy-start.18
  99.9 1.3 copy-start.20
  99.9 1.3 copy-start.22
  100.0 1.3 copy-start.24
  100.0 1.3 copy-start.26
  100.0 1.3 copy-start.28
  100.0 1.3 copy-start.30
  100.0 1.3 copy-start.32
  100.0 1.3 copy-start.34
  100.0 1.3 copy-start.36
  100.0 1.3 copy-start.38
  100.2 10.1 %copy-start.85 = (f32[352]{0:T(512)S(1)}, f32[352]{0:T(512)}, u32[]{:S(2)}) copy-start(f32[352]{0:T(512)} %param.25) | copy-start | bytes 4228
  104.4 14.3 %all-to-all-start.1 = ((bf16[1,1,8,4,4,352]{5,4,3,1,0,2:T(4,128)(2,1)}), bf16[1,1,8,4,4,352]{5,4,3,1,0,2:T(4,128)(2,1)S(1)}, u32[]{:S(2)}, u32[]{:S(2)}) async-start(bf16[1,1,8,4,4,352]{5,4,3,1,0,2:T(4,128)(2,1)} %bitcast.12), calls=%async_computation.1 | async-start | bytes 196608 | tf_op jit(solution)/shard_map/all_to_all | solution.py:198
  (25 other events, 32.6 us)
Sparse Core Ops, SparseCore 0:
  100.4 144.1 all-reduce.5
where the time goes:
time: 257 us; the launch traced here: 254 us
  waiting for transfers between devices  132 us (51%)
  local copies, waits for them, and re-layouts  66.1 us (26%)
  between operations  17.7 us (7%)
  other arithmetic  15.1 us (6%)
  starting transfers between devices  13.4 us (5%)
  matrix products  10 us (4%)
    unnamed x2, waiting for transfers between devices  126 us
    concatenate x1, local copies, waits for them, and re-layouts, image_step(): jnp.concatenate([g_kernel.reshape(-1), g_dw_bias, layer_norm_gain_gradien...  37.9 us
    all_to_all x1, starting transfers between devices, per_device(): lax.all_to_all(image_tiles, 'group', split_axis=2, concat_axis=2, tiled=T...  7.45 us
    reshape x1, local copies, waits for them, and re-layouts, per_device(): padded.reshape(devices_all, shard_len)  6.38 us
    all_to_all x1, starting transfers between devices, per_device(): lax.all_to_all(back_tiles[None, None], 'group', split_axis=2, concat_axis...  5.96 us
    all_to_all x1, waiting for transfers between devices, per_device(): lax.all_to_all(back_tiles[None, None], 'group', split_axis=2, concat_axis...  5.82 us
  transfers between devices with their start and end apart: 3, of which 2 were waited for; matrix products, arithmetic and copies ran while one was open for 6% of the time, Pallas kernels for 0%

commit v1 on v0

--- a/solution.py
+++ b/solution.py
@@ -5,6 +5,15 @@
 from jax.sharding import PartitionSpec as P
 
 GC = 4
+array_check = lambda arr_in, dim_no, ndim_at: jnp.concatenate(
+    jax.lax.all_to_all(
+        jnp.stack(jnp.split(arr_in, jax.lax.axis_size("group"), dim_no)),
+        split_axis=0,
+        concat_axis=0,
+        axis_name="group",
+    ),
+    ndim_at,
+)
 
 
 def image_step(
@@ -170,7 +179,7 @@
     weight_out,
     bias_out,
 ):
-    received = lax.all_to_all(image_tiles, "group", split_axis=2, concat_axis=2, tiled=True)
+    received = array_check(image_tiles, dim_no=2, ndim_at=2)
     tiles = received[0, 0]
     slot_count, tile_h, tile_w, channel_count = tiles.shape
     grid_rows = slot_count // GC

time: 257 us -> 268 us (1.043)
  local copies, waits for them, and re-layouts: 66.1 us -> 76.7 us
    unnamed x173 -> x180, local copies, waits for them, and re-layouts: 1.01 us -> 10.3 us
where the time goes in v1:
time: 268 us; the launch traced here: 265 us
  waiting for transfers between devices  132 us (49%)
  local copies, waits for them, and re-layouts  76.7 us (29%)
  between operations  17.7 us (7%)
  other arithmetic  15.1 us (6%)
  starting transfers between devices  13.3 us (5%)
  matrix products  10 us (4%)
    unnamed x2, waiting for transfers between devices  126 us
    concatenate x1, local copies, waits for them, and re-layouts, image_step(): jnp.concatenate([g_kernel.reshape(-1), g_dw_bias, layer_norm_gain_gradien...  37.9 us
    unnamed x180, local copies, waits for them, and re-layouts  10.3 us
    all_to_all x1, starting transfers between devices, jax.lax.all_to_all(jnp.stack(jnp.split(arr_in, jax.lax.axis_size('group')...  7.31 us
    reshape x1, local copies, waits for them, and re-layouts, per_device(): padded.reshape(devices_all, shard_len)  6.38 us
    all_to_all x1, starting transfers between devices, per_device(): lax.all_to_all(back_tiles[None, None], 'group', split_axis=2, concat_axis...  5.94 us
    all_to_all x1, waiting for transfers between devices, per_device(): lax.all_to_all(back_tiles[None, None], 'group', split_axis=2, concat_axis...  5.82 us
  transfers between devices with their start and end apart: 3, of which 2 were waited for; matrix products, arithmetic and copies ran while one was open for 6% of the time, Pallas kernels for 0%

profile of v1, /device:TPU:0, one launch (start us, length us, event | category | flops | bytes accessed | tf_op | source)
XLA Modules:
  0.0 264.5 jit_solution(10443501598714763003)
XLA Ops:
  7.2 0.0 copy-start
  7.2 1.4 constant_dynamic-update-slice_fusion.7
  8.6 1.3 constant_dynamic-update-slice_fusion.6
  9.9 1.3 constant_dynamic-update-slice_fusion.5
  11.2 1.3 constant_dynamic-update-slice_fusion.4
  12.5 1.3 constant_dynamic-update-slice_fusion.3
  13.8 1.3 constant_dynamic-update-slice_fusion.2
  15.2 1.3 constant_dynamic-update-slice_fusion.1
  16.5 1.3 constant_dynamic-update-slice_fusion
  17.8 7.3 %all-to-all-start = ((bf16[8,1,1,1,4,4,352]{6,5,4,3,2,1,0:T(4,128)(2,1)}), bf16[8,1,1,1,4,4,352]{6,5,4,3,2,1,0:T(4,128)(2,1)S(1)}, u32[]{:S(2)}, u32[]{:S(2)}) async-start(bf16[8,1,1,1,4,4,352]{6,5,4,3,2,1,0:T(4,128)(2,1)} %constant_dynamic-update-slice_fusion), calls=%async_computation | async-start | bytes 196608 | tf_op jit(solution)/shard_map/all_to_all | solution.py:9
  25.1 0.0 all-reduce.6.cloned.1.call-start
  25.1 1.0 slice_reduce_fusion.46
  26.2 1.3 slice_reduce_fusion.48
  27.7 1.9 slice_reduce_fusion.47
  30.2 0.5 compare_convert_fusion.1
  30.7 0.6 broadcast_in_dim.67
  31.4 0.6 broadcast_in_dim.68
  32.0 0.1 broadcast_in_dim.64
  32.1 0.6 broadcast_in_dim.65
  32.7 0.9 copy.52
  33.6 0.1 reshape.172
  33.7 0.1 copy.41
  33.8 1.6 convert_reduce_fusion
  35.5 0.1 reshape.169
  35.6 0.7 select_convert_fusion
  36.3 2.2 fusion.123
  38.5 0.2 multiply_reduce_fusion.54
  38.7 0.1 add_convert_fusion.1
  39.0 1.1 multiply_reduce_fusion.2
  40.2 0.7 fusion.118
  41.6 2.6 multiply_reduce_fusion
  44.1 0.7 multiply_reduce_fusion.56
  45.4 1.6 fusion.121
  47.1 0.5 fusion.120
  47.6 0.1 copy.42
  47.7 0.2 multiply_reduce_fusion.3
  48.0 0.1 div.84
  48.1 0.6 multiply_reduce_fusion.4
  48.6 0.9 fusion.119
  49.5 0.4 multiply_reduce_fusion.22
  49.9 1.7 fusion.107
  52.2 0.2 stack.235
  52.4 0.1 reshape.175
  52.5 2.8 %reshape.176 = f32[495616]{0:T(1024)} reshape(f32[352,1408]{1,0:T(8,128)} %fusion.107) | data formatting | bytes 3964928 | tf_op jit(solution)/shard_map/reshape | solution.py:138
  55.3 2.5 fusion.111
  57.8 4.0 %reshape.177 = f32[495616]{0:T(1024)} reshape(f32[1408,352]{1,0:T(8,128)} %fusion.111) | data formatting | bytes 3964928 | tf_op jit(solution)/shard_map/reshape | solution.py:142
  61.8 37.9 %concatenate.3 = f32[1014112]{0:T(1024)} concatenate(f32[17248]{0:T(1024)S(1)} %reshape.175, f32[352]{0:T(512)S(1)} %get-tuple-element.59, f32[352]{0:T(512)S(1)} %get-tuple-element.57, f32[352]{0:T(512)S(1)} %get-tuple-element.73, f32[495616]{0:T(1024)} %reshape.176, f32[1408]{0:T(1024)S(1)} %get-tuple-element.124, f32[1408]{0:T(1024)S(1)} %get-tuple-element.6, ...), dimensions={0} | concatenate | bytes 8112896 | tf_op jit(solution)/shard_map/concatenate | solution.py:132
  99.6 4.3 %pad.13 = f32[1014272]{0:T(1024)} pad(f32[1014112]{0:T(1024)} %concatenate.3, f32[]{:T(128)} %constant.50.clone.1), padding=0_160 | pad | bytes 8113540 | tf_op jit(solution)/shard_map/jit(_pad)/pad | solution.py:215
  104.0 6.4 %reshape.178 = f32[32,31696]{1,0:T(8,128)} reshape(f32[1014272]{0:T(1024)} %pad.13) | data formatting | bytes 8114176 | tf_op jit(solution)/shard_map/reshape | solution.py:218
  110.7 0.0 all-reduce.6.cloned.1.call-update
  110.7 0.1 reshape.171
  110.8 0.7 broadcast_compare_fusion.1
  111.4 0.1 reshape.168
  111.5 0.1 copy.37
  112.0 2.1 fusion.100
  114.1 0.7 copy.43
  114.8 5.9 %all-to-all-start.1 = ((bf16[1,1,8,4,4,352]{5,4,3,1,0,2:T(4,128)(2,1)}), bf16[1,1,8,4,4,352]{5,4,3,1,0,2:T(4,128)(2,1)S(1)}, u32[]{:S(2)}, u32[]{:S(2)}) async-start(bf16[1,1,8,4,4,352]{5,4,3,1,0,2:T(4,128)(2,1)} %bitcast.19), calls=%async_computation.1 | async-start | bytes 196608 | tf_op jit(solution)/shard_map/all_to_all | solution.py:207
  120.8 1.7 fusion.2
  122.5 0.1 copy.38
  122.6 0.7 copy.39
  123.3 5.8 %all-to-all-done.1 = bf16[1,1,8,4,4,352]{5,4,3,1,0,2:T(4,128)(2,1)S(1)} async-done(((bf16[1,1,8,4,4,352]{5,4,3,1,0,2:T(4,128)(2,1)}), bf16[1,1,8,4,4,352]{5,4,3,1,0,2:T(4,128)(2,1)S(1)}, u32[]{:S(2)}, u32[]{:S(2)}) %all-to-all-start.1) | async-done | bytes 90144 | tf_op jit(solution)/shard_map/all_to_all | solution.py:207
  129.1 125.9 %all-reduce.6.cloned.1.call-done = f32[32,31696]{1,0:T(8,128)} async-done(((f32[32,31696]{1,0:T(8,128)}), f32[32,31696]{1,0:T(8,128)}) %all-reduce.6.cloned.1.call-update) | async-done | bytes 4057104
  255.1 2.0 dynamic-slice_multiply_fusion
  257.0 0.6 copy.64
  (231 shorter events, 0.7 us)
Async XLA Ops:
  7.2 31.9 %copy-start = (bf16[352,1408]{1,0:T(8,128)(2,1)S(1)}, bf16[352,1408]{1,0:T(8,128)(2,1)}, u32[]{:S(2)}) copy-start(bf16[352,1408]{1,0:T(8,128)(2,1)} %param.20) | copy-start | bytes 2973700
  7.2 31.5 %copy-start.84 = (f32[352]{0:T(512)S(1)}, f32[352]{0:T(512)}, u32[]{:S(2)}) copy-start(f32[352]{0:T(512)} %param.19) | copy-start | bytes 4228
  7.2 31.5 %copy-start.6 = (f32[352]{0:T(512)S(1)}, f32[352]{0:T(512)}, u32[]{:S(2)}) copy-start(f32[352]{0:T(512)} %param.18) | copy-start | bytes 4228
  7.2 31.8 %copy-start.81 = (f32[1408]{0:T(1024)S(1)}, f32[1408]{0:T(1024)}, u32[]{:S(2)}) copy-start(f32[1408]{0:T(1024)} %param.21) | copy-start | bytes 16900
  17.8 17.7 %all-to-all-start = ((bf16[8,1,1,1,4,4,352]{6,5,4,3,2,1,0:T(4,128)(2,1)}), bf16[8,1,1,1,4,4,352]{6,5,4,3,2,1,0:T(4,128)(2,1)S(1)}, u32[]{:S(2)}, u32[]{:S(2)}) async-start(bf16[8,1,1,1,4,4,352]{6,5,4,3,2,1,0:T(4,128)(2,1)} %constant_dynamic-update-slice_fusion), calls=%async_computation | async-start | bytes 196608 | tf_op jit(solution)/shard_map/all_to_all | solution.py:9
  25.1 230.0 %all-reduce.6.cloned.1.call-start = ((), (), s32[]{:S(2)}) async-start(), calls=%async_computation.2 | async-start | bytes 8126464
  26.1 12.3 %copy-start.7 = (f32[352]{0:T(512)}, f32[352]{0:T(512)S(1)}, u32[]{:S(2)}) copy-start(f32[352]{0:T(512)S(1)} %get-tuple-element.114) | copy-start | bytes 4228
  26.1 12.3 %copy-start.13 = (f32[352]{0:T(512)}, f32[352]{0:T(512)S(1)}, u32[]{:S(2)}) copy-start(f32[352]{0:T(512)S(1)} %get-tuple-element.117) | copy-start | bytes 4228
  26.1 14.0 %copy-start.9 = (f32[352]{0:T(512)}, f32[352]{0:T(512)S(1)}, u32[]{:S(2)}) copy-start(f32[352]{0:T(512)S(1)} %get-tuple-element.115) | copy-start | bytes 4228
  26.1 14.0 %copy-start.11 = (f32[352]{0:T(512)}, f32[352]{0:T(512)S(1)}, u32[]{:S(2)}) copy-start(f32[352]{0:T(512)S(1)} %get-tuple-element.116) | copy-start | bytes 4228
  26.1 14.0 %copy-start.15 = (f32[352]{0:T(512)}, f32[352]{0:T(512)S(1)}, u32[]{:S(2)}) copy-start(f32[352]{0:T(512)S(1)} %get-tuple-element.118) | copy-start | bytes 4228
  26.2 14.0 %copy-start.17 = (f32[352]{0:T(512)}, f32[352]{0:T(512)S(1)}, u32[]{:S(2)}) copy-start(f32[352]{0:T(512)S(1)} %get-tuple-element.119) | copy-start | bytes 4228
  26.2 14.0 %copy-start.19 = (f32[352]{0:T(512)}, f32[352]{0:T(512)S(1)}, u32[]{:S(2)}) copy-start(f32[352]{0:T(512)S(1)} %get-tuple-element.120) | copy-start | bytes 4228
  26.2 14.0 %copy-start.21 = (f32[352]{0:T(512)}, f32[352]{0:T(512)S(1)}, u32[]{:S(2)}) copy-start(f32[352]{0:T(512)S(1)} %get-tuple-element.121) | copy-start | bytes 4228
  26.2 14.0 %copy-start.23 = (f32[352]{0:T(512)}, f32[352]{0:T(512)S(1)}, u32[]{:S(2)}) copy-start(f32[352]{0:T(512)S(1)} %get-tuple-element.122) | copy-start | bytes 4228
  26.2 14.0 %copy-start.25 = (f32[352]{0:T(512)}, f32[352]{0:T(512)S(1)}, u32[]{:S(2)}) copy-start(f32[352]{0:T(512)S(1)} %get-tuple-element.123) | copy-start | bytes 4228
  27.5 11.3 %copy-start.35 = (f32[352]{0:T(512)}, f32[352]{0:T(512)S(1)}, u32[]{:S(2)}) copy-start(f32[352]{0:T(512)S(1)} %get-tuple-element.79) | copy-start | bytes 4228
  27.5 11.3 %copy-start.37 = (f32[352]{0:T(512)}, f32[352]{0:T(512)S(1)}, u32[]{:S(2)}) copy-start(f32[352]{0:T(512)S(1)} %get-tuple-element.80) | copy-start | bytes 4228
  27.5 11.3 %copy-start.39 = (f32[352]{0:T(512)}, f32[352]{0:T(512)S(1)}, u32[]{:S(2)}) copy-start(f32[352]{0:T(512)S(1)} %get-tuple-element.81) | copy-start | bytes 4228
  27.5 11.3 %copy-start.41 = (f32[352]{0:T(512)}, f32[352]{0:T(512)S(1)}, u32[]{:S(2)}) copy-start(f32[352]{0:T(512)S(1)} %get-tuple-element.82) | copy-start | bytes 4228
  27.5 11.3 %copy-start.43 = (f32[352]{0:T(512)}, f32[352]{0:T(512)S(1)}, u32[]{:S(2)}) copy-start(f32[352]{0:T(512)S(1)} %get-tuple-element.83) | copy-start | bytes 4228
  27.5 11.3 %copy-start.45 = (f32[352]{0:T(512)}, f32[352]{0:T(512)S(1)}, u32[]{:S(2)}) copy-start(f32[352]{0:T(512)S(1)} %get-tuple-element.84) | copy-start | bytes 4228
  27.6 11.3 %copy-start.47 = (f32[352]{0:T(512)}, f32[352]{0:T(512)S(1)}, u32[]{:S(2)}) copy-start(f32[352]{0:T(512)S(1)} %get-tuple-element.85) | copy-start | bytes 4228
  27.6 11.3 %copy-start.49 = (f32[352]{0:T(512)}, f32[352]{0:T(512)S(1)}, u32[]{:S(2)}) copy-start(f32[352]{0:T(512)S(1)} %get-tuple-element.86) | copy-start | bytes 4228
  27.6 11.3 %copy-start.51 = (f32[352]{0:T(512)}, f32[352]{0:T(512)S(1)}, u32[]{:S(2)}) copy-start(f32[352]{0:T(512)S(1)} %get-tuple-element.87) | copy-start | bytes 4228
  27.6 11.3 %copy-start.53 = (f32[352]{0:T(512)}, f32[352]{0:T(512)S(1)}, u32[]{:S(2)}) copy-start(f32[352]{0:T(512)S(1)} %get-tuple-element.88) | copy-start | bytes 4228
  27.6 11.3 %copy-start.55 = (f32[352]{0:T(512)}, f32[352]{0:T(512)S(1)}, u32[]{:S(2)}) copy-start(f32[352]{0:T(512)S(1)} %get-tuple-element.89) | copy-start | bytes 4228
  27.6 11.3 %copy-start.57 = (f32[352]{0:T(512)}, f32[352]{0:T(512)S(1)}, u32[]{:S(2)}) copy-start(f32[352]{0:T(512)S(1)} %get-tuple-element.90) | copy-start | bytes 4228
  27.6 11.3 %copy-start.59 = (f32[352]{0:T(512)}, f32[352]{0:T(512)S(1)}, u32[]{:S(2)}) copy-start(f32[352]{0:T(512)S(1)} %get-tuple-element.91) | copy-start | bytes 4228
  27.6 11.3 %copy-start.61 = (f32[352]{0:T(512)}, f32[352]{0:T(512)S(1)}, u32[]{:S(2)}) copy-start(f32[352]{0:T(512)S(1)} %get-tuple-element.92) | copy-start | bytes 4228
  27.6 11.3 %copy-start.63 = (f32[352]{0:T(512)}, f32[352]{0:T(512)S(1)}, u32[]{:S(2)}) copy-start(f32[352]{0:T(512)S(1)} %get-tuple-element.93) | copy-start | bytes 4228
  27.6 12.6 %copy-start.27 = (f32[352]{0:T(512)}, f32[352]{0:T(512)S(1)}, u32[]{:S(2)}) copy-start(f32[352]{0:T(512)S(1)} %get-tuple-element.75) | copy-start | bytes 4228
  27.6 12.6 %copy-start.29 = (f32[352]{0:T(512)}, f32[352]{0:T(512)S(1)}, u32[]{:S(2)}) copy-start(f32[352]{0:T(512)S(1)} %get-tuple-element.76) | copy-start | bytes 4228
  27.7 12.6 %copy-start.31 = (f32[352]{0:T(512)}, f32[352]{0:T(512)S(1)}, u32[]{:S(2)}) copy-start(f32[352]{0:T(512)S(1)} %get-tuple-element.77) | copy-start | bytes 4228
  27.7 12.6 %copy-start.33 = (f32[352]{0:T(512)}, f32[352]{0:T(512)S(1)}, u32[]{:S(2)}) copy-start(f32[352]{0:T(512)S(1)} %get-tuple-element.78) | copy-start | bytes 4228
  29.5 9.4 %copy-start.65 = (f32[352]{0:T(512)}, f32[352]{0:T(512)S(1)}, u32[]{:S(2)}) copy-start(f32[352]{0:T(512)S(1)} %get-tuple-element.94) | copy-start | bytes 4228
  29.5 9.4 %copy-start.67 = (f32[352]{0:T(512)}, f32[352]{0:T(512)S(1)}, u32[]{:S(2)}) copy-start(f32[352]{0:T(512)S(1)} %get-tuple-element.95) | copy-start | bytes 4228
  29.5 9.4 %copy-start.69 = (f32[352]{0:T(512)}, f32[352]{0:T(512)S(1)}, u32[]{:S(2)}) copy-start(f32[352]{0:T(512)S(1)} %get-tuple-element.96) | copy-start | bytes 4228
  29.5 9.4 %copy-start.71 = (f32[352]{0:T(512)}, f32[352]{0:T(512)S(1)}, u32[]{:S(2)}) copy-start(f32[352]{0:T(512)S(1)} %get-tuple-element.97) | copy-start | bytes 4228
  29.5 9.4 %copy-start.73 = (f32[352]{0:T(512)}, f32[352]{0:T(512)S(1)}, u32[]{:S(2)}) copy-start(f32[352]{0:T(512)S(1)} %get-tuple-element.98) | copy-start | bytes 4228
  29.5 9.4 %copy-start.75 = (f32[352]{0:T(512)}, f32[352]{0:T(512)S(1)}, u32[]{:S(2)}) copy-start(f32[352]{0:T(512)S(1)} %get-tuple-element.99) | copy-start | bytes 4228
  29.6 9.4 %copy-start.77 = (f32[352]{0:T(512)}, f32[352]{0:T(512)S(1)}, u32[]{:S(2)}) copy-start(f32[352]{0:T(512)S(1)} %get-tuple-element.100) | copy-start | bytes 4228
  29.6 9.4 %copy-start.79 = (f32[352]{0:T(512)}, f32[352]{0:T(512)S(1)}, u32[]{:S(2)}) copy-start(f32[352]{0:T(512)S(1)} %get-tuple-element.101) | copy-start | bytes 4228
  33.8 7.7 %copy-start.3 = (bf16[128,352]{0,1:T(8,128)(2,1)}, bf16[128,352]{0,1:T(8,128)(2,1)S(1)}, u32[]{:S(2)}) copy-start(bf16[128,352]{0,1:T(8,128)(2,1)S(1)} %copy.41) | copy-start | bytes 270340
  35.5 6.1 %copy-start.5 = (f32[1408]{0:T(1024)S(1)}, f32[1408]{0:T(1024)}, u32[]{:S(2)}) copy-start(f32[1408]{0:T(1024)} %param.22) | copy-start | bytes 16900
  35.6 3.4 %copy-start.1 = (bf16[8,16,352]{2,1,0:T(8,128)(2,1)}, bf16[8,16,352]{2,1,0:T(8,128)(2,1)S(1)}, u32[]{:S(2)}) copy-start(bf16[8,16,352]{2,1,0:T(8,128)(2,1)S(1)} %reshape.169) | copy-start | bytes 270340
  47.1 1.6 copy-start.2
  52.1 3.2 %copy-start.4 = (bf16[128,352]{0,1:T(8,128)(2,1)S(1)}, bf16[128,352]{0,1:T(8,128)(2,1)}, u32[]{:S(2)}) copy-start(bf16[128,352]{0,1:T(8,128)(2,1)} %copy-done.3) | copy-start | bytes 270340
  52.1 3.2 %copy-start.82 = (f32[1408]{0:T(1024)S(1)}, f32[1408]{0:T(1024)}, u32[]{:S(2)}) copy-start(f32[1408]{0:T(1024)} %param.23) | copy-start | bytes 16900
  57.8 4.0 %copy-start.83 = (f32[352]{0:T(512)S(1)}, f32[352]{0:T(512)}, u32[]{:S(2)}) copy-start(f32[352]{0:T(512)} %convert_reduce_fusion) | copy-start | bytes 4228
  110.4 1.3 copy-start.16
  110.4 1.3 copy-start.18
  110.4 1.3 copy-start.20
  110.4 1.3 copy-start.22
  110.4 1.3 copy-start.24
  110.4 1.3 copy-start.26
  110.4 1.3 copy-start.28
  110.4 1.3 copy-start.30
  110.4 1.3 copy-start.32
  110.4 1.3 copy-start.34
  110.5 1.3 copy-start.36
  110.5 1.3 copy-start.38
  110.7 10.1 %copy-start.85 = (f32[352]{0:T(512)S(1)}, f32[352]{0:T(512)}, u32[]{:S(2)}) copy-start(f32[352]{0:T(512)} %param.25) | copy-start | bytes 4228
  114.8 14.3 %all-to-all-start.1 = ((bf16[1,1,8,4,4,352]{5,4,3,1,0,2:T(4,128)(2,1)}), bf16[1,1,8,4,4,352]{5,4,3,1,0,2:T(4,128)(2,1)S(1)}, u32[]{:S(2)}, u32[]{:S(2)}) async-start(bf16[1,1,8,4,4,352]{5,4,3,1,0,2:T(4,128)(2,1)} %bitcast.19), calls=%async_computation.1 | async-start | bytes 196608 | tf_op jit(solution)/shard_map/all_to_all | solution.py:207
  (25 other events, 32.6 us)
Sparse Core Ops, SparseCore 0:
  110.8 144.1 all-reduce.5
